TPU v7x, 32 devices: a whole 2x2x4 slice. The times are simulated.
32 devices in a mesh: lat: 2 (over core), prop: 16 (over z, y, x).
Axes of the slice: x: 2, y: 2, z: 4, core: 2. Of those that a mesh axis runs over, the one named last changes fastest.
Arguments:
- right_side: float32 [2, 3, 16, 64, 4, 128], P(None, None, None, 'prop', 'lat'), may hold values from -30 to 30
- start_field: float32 [2, 3, 16, 64, 4, 128], P(None, None, None, 'prop', 'lat'), may hold values from -1.75 to 1.75
- region: int32 [64, 4, 128], P('prop', 'lat'), may hold values from 0 to 7
- core_mask: int32 [64, 4, 128], P('prop', 'lat'), may hold values 0 or 1
- intensity: float32 [64, 4, 128], P('prop', 'lat'), may hold values from 0 to 4
- eps_lin: float32 [8], replicated, may hold values from 1 to 12
- eps_loss: float32 [8], replicated, may hold values from 0.1 to 3
- kerr_coef: float32 [8], replicated, may hold values from 0.2 to 1
Outputs:
- new_field: float32 [2, 3, 16, 64, 4, 128], P(None, None, None, 'prop', 'lat')
All inputs are finite; a program needn't handle non-finite values. No bound on the sum of `core_mask` on one device may be relied on, other than what follows from the above.
Results may differ from a plain program's by a relative error of at most 0.00002.
Values sent between devices are 32-bit elements; how exact they have to be, the bound alone decides.
A program may use at most 64 MiB of HBM per device.

v0:
```python
import jax
import jax.numpy as jnp
from jax import lax
from jax.sharding import PartitionSpec as P

wave_sq = 0.25
wave_shift = 0.02
loss_gain = 3.2
tiny = 1e-06


def extended(array, sides, width):
    for axis, dim in sides:
        size, length = (lax.axis_size(axis), array.shape[dim])
        up = [(i, (i + 1) % size) for i in range(size - 1)]
        down = [(j, i) for i, j in up]
        last = lax.slice_in_dim(array, length - width, length, axis=dim)
        first = lax.slice_in_dim(array, 0, width, axis=dim)
        before = lax.ppermute(last, axis, up)
        after = lax.ppermute(first, axis, down)
        array = jnp.concatenate([before, array, after], axis=dim)
    return array


def trimmed(values, direction):
    selector = [slice(None)] * (values.ndim - 3) + [slice(0, -1)] * 3
    if direction is not None:
        selector[values.ndim + direction] = slice(1, None)
    return values[tuple(selector)]


def advance(values, direction):
    return trimmed(values, direction) - trimmed(values, None)


def upper(values, direction):
    selector = [slice(None)] * (values.ndim - 3) + [slice(1, None)] * 3
    if direction is not None:
        selector[values.ndim + direction] = slice(0, -1)
    return values[tuple(selector)]


def retreat(values, direction):
    return upper(values, None) - upper(values, direction)


def curl_twice(padded):
    field_x = padded[:, 0]
    field_y = padded[:, 1]
    field_z = padded[:, 2]
    magnet_x = advance(field_z, -1) - advance(field_y, -3)
    magnet_y = advance(field_x, -3) - advance(field_z, -2)
    magnet_z = advance(field_y, -2) - advance(field_x, -1)
    result_x = retreat(magnet_z, -1) - retreat(magnet_y, -3)
    result_y = retreat(magnet_x, -3) - retreat(magnet_z, -2)
    result_z = retreat(magnet_y, -2) - retreat(magnet_x, -1)
    return jnp.stack([result_x, result_y, result_z], axis=1)


def apply_operator(values, padded, perm_real, perm_imag):
    curled = curl_twice(padded)
    real_part = values[0]
    imag_part = values[1]
    out_real = curled[0] - wave_sq * (perm_real * real_part - perm_imag * imag_part)
    out_imag = curled[1] - wave_sq * (perm_real * imag_part + perm_imag * real_part)
    return jnp.stack([out_real, out_imag])


def ascend(gain_real, gain_imag, forward_value, behind):
    return jnp.stack(
        [
            forward_value[0] + gain_real * behind[0] - gain_imag * behind[1],
            forward_value[1] + gain_real * behind[1] + gain_imag * behind[0],
        ]
    )


def solve_batched(line_data, diag_real, diag_imag):
    depth = line_data.shape[3]
    lines_count = line_data.shape[4] * line_data.shape[5]
    moved = jnp.moveaxis(line_data, 3, 0)
    moved_shape = moved.shape
    rows = moved.reshape((depth, 2, -1))
    repeats = rows.shape[2] // lines_count
    plane_real = diag_real.reshape((depth, lines_count))
    plane_imag = diag_imag.reshape((depth, lines_count))
    unroll_count = min(16, depth)

    def gain_step(carried, element):
        gain_real, gain_imag = carried
        diag_now_real, diag_now_imag = element
        denom_real = diag_now_real - gain_real
        denom_imag = diag_now_imag - gain_imag
        magnitude = denom_real * denom_real + denom_imag * denom_imag
        new_real = denom_real / magnitude
        new_imag = -denom_imag / magnitude
        return ((new_real, new_imag), (new_real, new_imag))

    zero_line = jnp.zeros((lines_count,), jnp.float32)
    unused, (gains_real, gains_imag) = lax.scan(
        gain_step, (zero_line, zero_line), (plane_real, plane_imag), unroll=unroll_count
    )
    wide_real = jnp.tile(gains_real, (1, repeats))
    wide_imag = jnp.tile(gains_imag, (1, repeats))

    def front_step(previous, element):
        gain_real, gain_imag, source = element
        sum_real = source[0] + previous[0]
        sum_imag = source[1] + previous[1]
        updated = jnp.stack(
            [
                gain_real * sum_real - gain_imag * sum_imag,
                gain_real * sum_imag + gain_imag * sum_real,
            ]
        )
        return (updated, updated)

    unused, fronts = lax.scan(
        front_step, jnp.zeros_like(rows[0]), (wide_real, wide_imag, rows), unroll=unroll_count
    )

    def back_step(behind, element):
        gain_real, gain_imag, forward_value = element
        new_value = ascend(gain_real, gain_imag, forward_value, behind)
        return (new_value, new_value)

    unused, values = lax.scan(
        back_step,
        jnp.zeros_like(rows[0]),
        (wide_real, wide_imag, fronts),
        reverse=True,
        unroll=unroll_count,
    )
    return jnp.moveaxis(values.reshape(moved_shape), 0, 3)


def per_device(right_side, start_field, region, core_mask, intensity, eps_lin, eps_loss, kerr_coef):
    levels = jnp.arange(eps_lin.shape[0], dtype=jnp.int32)
    onehot = (region[None] == levels[:, None, None, None]).astype(jnp.float32)
    lin_cell = jnp.sum(onehot * eps_lin[:, None, None, None], axis=0)
    loss_cell = jnp.sum(onehot * eps_loss[:, None, None, None], axis=0)
    kerr_cell = jnp.sum(onehot * kerr_coef[:, None, None, None], axis=0)
    perm_real = lin_cell + core_mask.astype(jnp.float32) * kerr_cell * intensity
    planes = right_side.shape[3]
    total_planes = planes * lax.axis_size("prop")
    diag_real = 2.0 - wave_shift * perm_real
    diag_imag = loss_gain / total_planes * loss_cell

    def operate(values):
        padded = extended(values, (("lat", 4), ("prop", 3)), 1)
        padded = jnp.pad(padded, ((0, 0), (0, 0), (0, 0), (0, 0), (0, 0), (1, 1)))
        return apply_operator(values, padded, perm_real, loss_cell)

    residual = right_side - operate(start_field)
    coeffs = jnp.stack([diag_real, diag_imag])
    line_diag = lax.all_to_all(coeffs, "prop", split_axis=3, concat_axis=1, tiled=True)
    solved = solve_batched(
        lax.all_to_all(residual, "prop", split_axis=5, concat_axis=3, tiled=True),
        line_diag[0],
        line_diag[1],
    )
    precond = lax.all_to_all(solved, "prop", split_axis=3, concat_axis=5, tiled=True)
    image_field = operate(precond)
    cross_sum = jnp.sum(residual * image_field, axis=(0, 1, 3, 4, 5))
    self_sum = jnp.sum(image_field * image_field, axis=(0, 1, 3, 4, 5))
    totals = lax.psum((cross_sum, self_sum), ("lat", "prop"))
    step_size = totals[0] / (totals[1] + tiny)
    return start_field + step_size[None, None, :, None, None, None] * precond


def solution(mesh):
    placed = (
        P(None, None, None, "prop", "lat", None),
        P(None, None, None, "prop", "lat", None),
        P("prop", "lat", None),
        P("prop", "lat", None),
        P("prop", "lat", None),
        P(),
        P(),
        P(),
    )
    return jax.shard_map(
        per_device,
        mesh=mesh,
        in_specs=placed,
        out_specs=P(None, None, None, "prop", "lat", None),
        check_vma=False,
    )
```

profile of v0, /device:TPU:0, one launch (start us, length us, event | category | flops | bytes accessed | tf_op | source)
XLA Modules:
  0.0 232.1 jit_solution(9379006360073458968)
XLA Ops:
  0.0 1.1 copy.262
  1.2 2.4 %collective-permute-start = (f32[2,3,16,4,1,128]{5,2,4,3,1,0:T(8,128)S(1)}, f32[2,3,16,4,1,128]{5,2,4,3,1,0:T(8,128)S(1)}, u32[]{:S(2)}, u32[]{:S(2)}) collective-permute-start(f32[2,3,16,4,1,128]{5,2,4,3,1,0:T(8,128)S(1)} %get-tuple-element.468), channel_id=1, source_target_pairs={{0,16},{1,17},{2,18},{3,19},{4,20},{5,21},{6,22},{7,23},{8,24},{9,... | collective-permute-start | bytes 589832 | tf_op jit(solution)/shard_map/ppermute | solution.py:19
  6.3 7.7 %all-to-all-start = ((f32[16,1,128]{2,1,0:T(1,128)}), f32[16,1,128]{2,1,0:T(1,128)S(1)}, u32[]{:S(2)}, u32[]{:S(2)}) async-start(f32[16,1,128]{2,1,0:T(1,128)} %reshape.3988), calls=%async_computation | async-start | bytes 16384 | tf_op jit(solution)/shard_map/all_to_all | solution.py:156
  14.0 1.3 collective-permute-start.1
  15.4 5.9 %all-to-all-done = f32[16,1,128]{2,1,0:T(1,128)S(1)} async-done(((f32[16,1,128]{2,1,0:T(1,128)}), f32[16,1,128]{2,1,0:T(1,128)S(1)}, u32[]{:S(2)}, u32[]{:S(2)}) %all-to-all-start) | async-done | bytes 8224 | tf_op jit(solution)/shard_map/all_to_all | solution.py:156
  23.6 2.5 %collective-permute-start.2 = (f32[2,3,16,1,4,128]{5,2,4,3,1,0:T(8,128)S(1)}, f32[2,3,16,1,4,128]{5,2,4,3,1,0:T(8,128)S(1)}, u32[]{:S(2)}, u32[]{:S(2)}) collective-permute-start(f32[2,3,16,1,4,128]{5,2,4,3,1,0:T(8,128)S(1)} %get-tuple-element.459), channel_id=1, source_target_pairs={{0,1},{1,2},{2,3},{3,4},{4,5},{5,6},{6,7},{7,8},{8,9},{9,10},{10,1... | collective-permute-start | bytes 589832 | tf_op jit(solution)/shard_map/ppermute | solution.py:19
  26.1 1.3 collective-permute-start.3
  29.3 5.3 %collective-permute-done.3 = f32[2,3,16,1,4,128]{5,2,4,3,1,0:T(8,128)S(1)} collective-permute-done((f32[2,3,16,1,4,128]{5,2,4,3,1,0:T(8,128)S(1)}, f32[2,3,16,1,4,128]{5,2,4,3,1,0:T(8,128)S(1)}, u32[]{:S(2)}, u32[]{:S(2)}) %collective-permute-start.3) | collective-permute-done | bytes 196640 | tf_op jit(solution)/shard_map/ppermute | solution.py:20
  37.2 2.2 copy.238
  39.4 4.9 %reshape.3990 = f32[16,1,6144]{2,1,0:T(1,128)} reshape(f32[128,2,3,4,2,16]{5,4,3,2,1,0:T(2,128)S(1)} %bitcast.1633) | data formatting | bytes 786432
  44.3 4.6 %all-to-all-start.1 = ((f32[16,1,6144]{2,1,0:T(1,128)}), f32[16,1,6144]{2,1,0:T(1,128)S(1)}, u32[]{:S(2)}, u32[]{:S(2)}) async-start(f32[16,1,6144]{2,1,0:T(1,128)} %reshape.3990), calls=%async_computation.1 | async-start | bytes 786432 | tf_op jit(solution)/shard_map/all_to_all | solution.py:158
  49.0 44.4 %while.47 = (s32[]{:T(128)}, f32[16]{0:T(128)S(1)}, f32[16]{0:T(128)S(1)}, f32[4,16,16]{2,1,0:T(8,128)S(1)}, f32[4,16,16]{2,1,0:T(8,128)S(1)}, /*index=5*/f32[4,...) while((s32[]{:T(128)}, f32[16]{0:T(128)S(1)}, ...), condition=%wide.region_4.5_spmd.clone, body=%wide.region_3.4_spmd.clone.sunk | while | flops 2482 | bytes 45483 | solution.py:100
  94.9 2.4 %reduce.1 = f32[16,6144]{1,0:T(8,128)} reduce(f32[16,1,6144]{2,1,0:T(1,128)S(1)} %all-to-all-done.1, f32[]{:T(128)} %broadcast.160), dimensions={1}, to_apply=%all_to_all.40.reduce_sub_computation | reduce | bytes 786436 | tf_op jit(solution)/shard_map/all_to_all | solution.py:158
  97.3 5.3 %reshape.3991 = f32[128,2,3,4,2,16]{5,4,3,2,1,0:T(2,128)S(1)} reshape(f32[16,6144]{1,0:T(8,128)} %reduce.1) | data formatting | bytes 786432
  102.5 0.9 copy.280
  103.9 2.3 copy.241
  106.2 2.5 %reshape_reshape.6 = f32[4,16,2,768]{1,0,3,2:T(4,128)S(1)} reshape(f32[64,2,3,16,2,8]{0,5,4,3,2,1:T(8,128)} %copy.241) | data formatting | bytes 786432 | tf_op jit(solution)/shard_map/reshape;reshape | solution.py:118
  108.7 2.1 copy.242
  110.9 9.7 %while.45 = (s32[]{:T(128)}, f32[2,768]{1,0:T(2,128)S(1)}, f32[4,16,2,768]{3,2,1,0:T(2,128)S(1)}, f32[4,16,768]{2,1,0:T(8,128)S(1)}, f32[4,16,2,768]{3,2,1,0:T(2...) while((s32[]{:T(128)}, f32[2,768]{1,0:T(2,128)S(1)}, ...), condition=%wide.region_6.7_spmd, body=%wide.region_5.6_spmd.sunk | while | flops 124432 | bytes 719313 | solution.py:118
  110.9 1.3 multiply_subtract_fusion.32
  113.4 1.3 multiply_subtract_fusion.32
  115.8 1.3 multiply_subtract_fusion.32
  118.2 1.3 multiply_subtract_fusion.32
  120.8 2.9 %while.46 = (s32[]{:T(128)}, f32[2,768]{1,0:T(2,128)S(1)}, f32[4,16,2,768]{3,2,1,0:T(2,128)S(1)}, f32[4,16,2,768]{3,2,1,0:T(2,128)S(1)}, f32[4,16,768]{2,1,0:T(8...) while((s32[]{:T(128)}, f32[2,768]{1,0:T(2,128)S(1)}, ...), condition=%wide.region_8.9_spmd, body=%wide.region_7.8_spmd.sunk | while | flops 122897 | bytes 713185 | solution.py:127
  124.5 2.8 %copy.243 = f32[4,16,2,768]{1,0,3,2:T(4,128)S(1)} copy(f32[4,16,2,768]{3,2,1,0:T(2,128)} %copy-done.8) | data formatting | bytes 786432 | tf_op jit(solution)/shard_map/while | solution.py:127
  127.3 2.2 reshape_reshape.7
  129.5 2.7 %copy.244 = f32[2,3,16,64,2,8]{2,5,4,1,0,3:T(8,128)S(1)} copy(f32[2,3,16,64,2,8]{3,5,4,2,1,0:T(8,128)} %bitcast.1638) | data formatting | bytes 786432 | tf_op jit(solution)/shard_map/transpose | solution.py:134
  132.2 1.1 reshape.3992
  133.3 18.0 %all_to_all.51 = f32[16,1,6144]{2,1,0:T(1,128)S(1)} all-to-all(f32[16,1,6144]{2,1,0:T(1,128)S(1)} %reshape.3992), channel_id=1, replica_groups=mesh['lat'=2,'prop'=16] {'prop'}, dimensions={0} | all-to-all | bytes 786432 | tf_op jit(solution)/shard_map/all_to_all | solution.py:162
  151.3 1.5 reduce.2
  152.9 1.1 reshape.3993
  153.9 2.1 copy.245
  156.6 2.3 copy.279
  158.9 1.9 fusion.385
  160.8 1.1 copy.249
  161.9 2.7 %copy.247 = f32[2,3,16,4,1,128]{5,2,4,3,1,0:T(8,128)} copy(f32[2,3,16,4,1,128]{2,5,4,3,1,0:T(8,128)} %get-tuple-element.439) | data formatting | bytes 393216 | tf_op jit(solution)/shard_map/slice | solution.py:17
  164.6 2.0 collective-permute-start.4
  166.5 2.5 %copy.248 = f32[2,3,16,4,1,128]{5,2,4,3,1,0:T(8,128)} copy(f32[2,3,16,4,1,128]{2,5,4,3,1,0:T(8,128)} %get-tuple-element.440) | data formatting | bytes 393216 | tf_op jit(solution)/shard_map/slice | solution.py:18
  169.1 1.3 collective-permute-start.5
  170.7 1.9 collective-permute-done.5
  172.6 1.7 pad_maximum_fusion.7
  174.3 3.2 %collective-permute-start.6 = (f32[2,3,16,1,4,128]{5,2,4,3,1,0:T(8,128)}, f32[2,3,16,1,4,128]{5,2,4,3,1,0:T(8,128)}, u32[]{:S(2)}, u32[]{:S(2)}) collective-permute-start(f32[2,3,16,1,4,128]{5,2,4,3,1,0:T(8,128)} %get-tuple-element.454), channel_id=1, source_target_pairs={{0,1},{1,2},{2,3},{3,4},{4,5},{5,6},{6,7},{7,8},{8,9},{9,10},{10,1... | collective-permute-start | bytes 589832 | tf_op jit(solution)/shard_map/ppermute | solution.py:19
  177.4 1.3 collective-permute-start.7
  179.1 1.1 copy.256
  181.5 6.4 %collective-permute-done.7 = f32[2,3,16,1,4,128]{5,2,4,3,1,0:T(8,128)} collective-permute-done((f32[2,3,16,1,4,128]{5,2,4,3,1,0:T(8,128)}, f32[2,3,16,1,4,128]{5,2,4,3,1,0:T(8,128)}, u32[]{:S(2)}, u32[]{:S(2)}) %collective-permute-start.7) | collective-permute-done | bytes 196640 | tf_op jit(solution)/shard_map/ppermute | solution.py:20
  187.9 1.9 select_maximum_fusion
  192.0 39.0 %all-reduce.2 = (f32[16]{0:T(128)S(1)}, f32[16]{0:T(128)S(1)}) all-reduce(f32[16]{0:T(128)S(1)} %get-tuple-element.262, f32[16]{0:T(128)S(1)} %get-tuple-element.261), channel_id=1, replica_groups=mesh['lat'=2,'prop'=16] {'lat','prop'}, use_global_device_ids=true, to_apply=%region_10.11 | all-reduce | flops 32 | bytes 256 | tf_op jit(solution)/shard_map/psum | solution.py:166
  231.1 0.9 copy.263
  (311 shorter events, 68.2 us)
Async XLA Ops:
  0.0 23.5 %copy-start.2 = (f32[2,3,16,4,2,128]{5,4,3,2,1,0:T(2,128)S(1)}, f32[2,3,16,4,2,128]{5,4,3,2,1,0:T(2,128)}, u32[]{:S(2)}) copy-start(f32[2,3,16,4,2,128]{5,4,3,2,1,0:T(2,128)} %param.15) | copy-start | bytes 1179652
  1.2 22.2 %collective-permute-start = (f32[2,3,16,4,1,128]{5,2,4,3,1,0:T(8,128)S(1)}, f32[2,3,16,4,1,128]{5,2,4,3,1,0:T(8,128)S(1)}, u32[]{:S(2)}, u32[]{:S(2)}) collective-permute-start(f32[2,3,16,4,1,128]{5,2,4,3,1,0:T(8,128)S(1)} %get-tuple-element.468), channel_id=1, source_target_pairs={{0,16},{1,17},{2,18},{3,19},{4,20},{5,21},{6,22},{7,23},{8,24},{9,... | collective-permute-start | bytes 589832 | tf_op jit(solution)/shard_map/ppermute | solution.py:19
  6.3 14.9 %all-to-all-start = ((f32[16,1,128]{2,1,0:T(1,128)}), f32[16,1,128]{2,1,0:T(1,128)S(1)}, u32[]{:S(2)}, u32[]{:S(2)}) async-start(f32[16,1,128]{2,1,0:T(1,128)} %reshape.3988), calls=%async_computation | async-start | bytes 16384 | tf_op jit(solution)/shard_map/all_to_all | solution.py:156
  14.0 9.5 %collective-permute-start.1 = (f32[2,3,16,4,1,128]{5,2,4,3,1,0:T(8,128)S(1)}, f32[2,3,16,4,1,128]{5,2,4,3,1,0:T(8,128)S(1)}, u32[]{:S(2)}, u32[]{:S(2)}) collective-permute-start(f32[2,3,16,4,1,128]{5,2,4,3,1,0:T(8,128)S(1)} %get-tuple-element.467), channel_id=1, source_target_pairs={{16,0},{17,1},{18,2},{19,3},{20,4},{21,5},{22,6},{23,7},{24,8},{25... | collective-permute-start | bytes 589832 | tf_op jit(solution)/shard_map/ppermute | solution.py:20
  23.6 5.7 %collective-permute-start.2 = (f32[2,3,16,1,4,128]{5,2,4,3,1,0:T(8,128)S(1)}, f32[2,3,16,1,4,128]{5,2,4,3,1,0:T(8,128)S(1)}, u32[]{:S(2)}, u32[]{:S(2)}) collective-permute-start(f32[2,3,16,1,4,128]{5,2,4,3,1,0:T(8,128)S(1)} %get-tuple-element.459), channel_id=1, source_target_pairs={{0,1},{1,2},{2,3},{3,4},{4,5},{5,6},{6,7},{7,8},{8,9},{9,10},{10,1... | collective-permute-start | bytes 589832 | tf_op jit(solution)/shard_map/ppermute | solution.py:19
  26.1 8.5 %collective-permute-start.3 = (f32[2,3,16,1,4,128]{5,2,4,3,1,0:T(8,128)S(1)}, f32[2,3,16,1,4,128]{5,2,4,3,1,0:T(8,128)S(1)}, u32[]{:S(2)}, u32[]{:S(2)}) collective-permute-start(f32[2,3,16,1,4,128]{5,2,4,3,1,0:T(8,128)S(1)} %get-tuple-element.460), channel_id=1, source_target_pairs={{1,0},{2,1},{3,2},{4,3},{5,4},{6,5},{7,6},{8,7},{9,8},{10,9},{11,1... | collective-permute-start | bytes 589832 | tf_op jit(solution)/shard_map/ppermute | solution.py:20
  35.9 1.2 copy-start.9
  36.3 0.7 copy-start.4
  36.3 0.7 copy-start.6
  39.4 9.6 %copy-start.13 = (f32[4,16,16]{2,1,0:T(8,128)S(1)}, f32[4,16,16]{2,1,0:T(8,128)}, u32[]{:S(2)}) copy-start(f32[4,16,16]{2,1,0:T(8,128)} %custom-call.5) | copy-start | bytes 12292
  39.4 9.6 %copy-start.14 = (f32[4,16,16]{2,1,0:T(8,128)S(1)}, f32[4,16,16]{2,1,0:T(8,128)}, u32[]{:S(2)}) copy-start(f32[4,16,16]{2,1,0:T(8,128)} %custom-call.6) | copy-start | bytes 12292
  44.3 50.6 %all-to-all-start.1 = ((f32[16,1,6144]{2,1,0:T(1,128)}), f32[16,1,6144]{2,1,0:T(1,128)S(1)}, u32[]{:S(2)}, u32[]{:S(2)}) async-start(f32[16,1,6144]{2,1,0:T(1,128)} %reshape.3990), calls=%async_computation.1 | async-start | bytes 786432 | tf_op jit(solution)/shard_map/all_to_all | solution.py:158
  123.7 0.7 copy-start.8
  153.9 2.7 %copy-start = (f32[64,2,3,2,8,16]{5,4,3,2,1,0:T(8,128)}, f32[64,2,3,2,8,16]{5,4,3,2,1,0:T(8,128)S(1)}, u32[]{:S(2)}) copy-start(f32[64,2,3,2,8,16]{5,4,3,2,1,0:T(8,128)S(1)} %reshape.3993) | copy-start | bytes 1179652
  161.9 8.5 %copy-start.1 = (f32[2,3,16,64,2,8]{2,5,4,3,1,0:T(8,128)S(1)}, f32[2,3,16,64,2,8]{2,5,4,3,1,0:T(8,128)}, u32[]{:S(2)}) copy-start(f32[2,3,16,64,2,8]{2,5,4,3,1,0:T(8,128)} %copy.245) | copy-start | bytes 1179652
  164.6 6.2 %collective-permute-start.4 = (f32[2,3,16,4,1,128]{5,2,4,3,1,0:T(8,128)}, f32[2,3,16,4,1,128]{5,2,4,3,1,0:T(8,128)}, u32[]{:S(2)}, u32[]{:S(2)}) collective-permute-start(f32[2,3,16,4,1,128]{5,2,4,3,1,0:T(8,128)} %copy.247), channel_id=1, source_target_pairs={{0,16},{1,17},{2,18},{3,19},{4,20},{5,21},{6,22},{7,23},{8,24},{9,... | collective-permute-start | bytes 589832 | tf_op jit(solution)/shard_map/ppermute | solution.py:19
  169.1 3.5 %collective-permute-start.5 = (f32[2,3,16,4,1,128]{5,2,4,3,1,0:T(8,128)}, f32[2,3,16,4,1,128]{5,2,4,3,1,0:T(8,128)S(1)}, u32[]{:S(2)}, u32[]{:S(2)}) collective-permute-start(f32[2,3,16,4,1,128]{5,2,4,3,1,0:T(8,128)} %copy.248), channel_id=1, source_target_pairs={{16,0},{17,1},{18,2},{19,3},{20,4},{21,5},{22,6},{23,7},{24,8},{25... | collective-permute-start | bytes 589832 | tf_op jit(solution)/shard_map/ppermute | solution.py:20
  172.6 6.5 %copy-start.12 = (f32[2,3,16,4,1,128]{5,2,4,3,1,0:T(8,128)}, f32[2,3,16,4,1,128]{5,2,4,3,1,0:T(8,128)S(1)}, u32[]{:S(2)}) copy-start(f32[2,3,16,4,1,128]{5,2,4,3,1,0:T(8,128)S(1)} %collective-permute-done.5) | copy-start | bytes 589828
  174.3 7.2 %collective-permute-start.6 = (f32[2,3,16,1,4,128]{5,2,4,3,1,0:T(8,128)}, f32[2,3,16,1,4,128]{5,2,4,3,1,0:T(8,128)}, u32[]{:S(2)}, u32[]{:S(2)}) collective-permute-start(f32[2,3,16,1,4,128]{5,2,4,3,1,0:T(8,128)} %get-tuple-element.454), channel_id=1, source_target_pairs={{0,1},{1,2},{2,3},{3,4},{4,5},{5,6},{6,7},{7,8},{8,9},{9,10},{10,1... | collective-permute-start | bytes 589832 | tf_op jit(solution)/shard_map/ppermute | solution.py:19
  177.4 10.5 %collective-permute-start.7 = (f32[2,3,16,1,4,128]{5,2,4,3,1,0:T(8,128)}, f32[2,3,16,1,4,128]{5,2,4,3,1,0:T(8,128)}, u32[]{:S(2)}, u32[]{:S(2)}) collective-permute-start(f32[2,3,16,1,4,128]{5,2,4,3,1,0:T(8,128)} %get-tuple-element.455), channel_id=1, source_target_pairs={{1,0},{2,1},{3,2},{4,3},{5,4},{6,5},{7,6},{8,7},{9,8},{10,9},{11,1... | collective-permute-start | bytes 589832 | tf_op jit(solution)/shard_map/ppermute | solution.py:20
  190.4 0.9 copy-start.11
  190.4 1.0 copy-start.5
  190.4 1.1 copy-start.7
  190.5 1.3 copy-start.10
  190.5 40.5 %copy-start.3 = (f32[2,3,16,4,2,128]{5,4,3,2,1,0:T(2,128)S(1)}, f32[2,3,16,4,2,128]{5,4,3,2,1,0:T(2,128)}, u32[]{:S(2)}) copy-start(f32[2,3,16,4,2,128]{5,4,3,2,1,0:T(2,128)} %param.15) | copy-start | bytes 1179652
where the time goes:
time: 236 us; the launch traced here: 232 us
  other arithmetic  67.8 us (29%)
  local copies, waits for them, and re-layouts  57.5 us (24%)
  blocking collectives  57 us (24%)
  starting transfers between devices  27.5 us (12%)
  waiting for transfers between devices  20.7 us (9%)
    psum x1, blocking collectives, per_device(): totals = lax.psum((cross_sum, self_sum), ('lat', 'prop'))  39 us
    sub x28, other arithmetic, gain_step(): denom_imag = diag_now_imag - gain_imag  21.5 us
    sub x28, other arithmetic, gain_step(): denom_real = diag_now_real - gain_real  19.4 us
    all_to_all x1, blocking collectives, per_device(): lax.all_to_all(solved, 'prop', split_axis=3, concat_axis=5, tiled=True)  18 us
    unnamed x39, local copies, waits for them, and re-layouts  17.8 us
    ppermute x4, waiting for transfers between devices, extended(): after = lax.ppermute(first, axis, down)  13.6 us
    ppermute x4, starting transfers between devices, extended(): before = lax.ppermute(last, axis, up)  10.1 us
    all_to_all x1, starting transfers between devices, per_device(): lax.all_to_all(coeffs, 'prop', split_axis=3, concat_axis=1, tiled=True)  7.68 us
  transfers between devices with their start and end apart: 10, of which 6 were waited for; matrix products, arithmetic and copies ran while one was open for 25% of the time, Pallas kernels for 0%

commit v1 on v0

--- a/solution.py
+++ b/solution.py
@@ -7,6 +7,17 @@
 wave_shift = 0.02
 loss_gain = 3.2
 tiny = 1e-06
+
+
+def in_blocks(array, dim, devices):
+    before, after = (array.shape[:dim], array.shape[dim + 1 :])
+    return jnp.moveaxis(array.reshape(*before, devices, -1, *after), dim, 0)
+
+
+def laid_out(blocks, dim):
+    lengths = list(blocks.shape[1:])
+    lengths[dim] *= blocks.shape[0]
+    return jnp.moveaxis(blocks, 0, dim).reshape(lengths)
 
 
 def extended(array, sides, width):
@@ -159,7 +170,14 @@
         line_diag[0],
         line_diag[1],
     )
-    precond = lax.all_to_all(solved, "prop", split_axis=3, concat_axis=5, tiled=True)
+    length_2, index = (lax.axis_size("prop"), lax.axis_index("prop"))
+    blocks = in_blocks(solved, 3, length_2)
+    outs = [blocks[index]]
+    for step in range(1, length_2):
+        sent = blocks[index ^ step]
+        outs.append(lax.ppermute(sent, "prop", [(i_2, i_2 ^ step) for i_2 in range(length_2)]))
+    blocks = jnp.stack(outs)[index ^ jnp.arange(length_2)]
+    precond = laid_out(blocks, 5)
     image_field = operate(precond)
     cross_sum = jnp.sum(residual * image_field, axis=(0, 1, 3, 4, 5))
     self_sum = jnp.sum(image_field * image_field, axis=(0, 1, 3, 4, 5))

time: 236 us -> 304 us (1.29)
  starting transfers between devices: 27.5 us -> 77.2 us
  waiting for transfers between devices: 20.7 us -> 38.2 us
  local copies, waits for them, and re-layouts: 57.5 us -> 67.6 us
  blocking collectives: 57 us -> 48.5 us
    ppermute x0 -> x15, starting transfers between devices: none -> 48.3 us  [per_device(): lax.ppermute(sent, 'prop', [(i_2, i_2 ^ step) for i_2 in range(length_2)])]
    all_to_all x1 -> x0, blocking collectives: 18 us -> none  [per_device(): lax.all_to_all(solved, 'prop', split_axis=3, concat_axis=5, tiled=True)]
    ppermute x0 -> x15, waiting for transfers between devices: none -> 14.8 us  [per_device(): lax.ppermute(sent, 'prop', [(i_2, i_2 ^ step) for i_2 in range(length_2)])]
    psum x1, blocking collectives: 39 us -> 48.5 us  [per_device(): totals = lax.psum((cross_sum, self_sum), ('lat', 'prop'))]
    unnamed x39 -> x50, local copies, waits for them, and re-layouts: 17.8 us -> 27.1 us
    all_to_all x3 -> x0, local copies, waits for them, and re-layouts: 5.51 us -> none  [per_device(): lax.all_to_all(solved, 'prop', split_axis=3, concat_axis=5, tiled=True)]
  transfers between devices with their start and end apart: 10 -> 25, of which waited for: 6 -> 14; matrix products, arithmetic and copies ran while one was open for 25% -> 23% of each run, Pallas kernels for 0% -> 0%
where the time goes in v1:
time: 304 us; the launch traced here: 300 us
  starting transfers between devices  77.2 us (25%)
  local copies, waits for them, and re-layouts  67.6 us (22%)
  other arithmetic  67.2 us (22%)
  blocking collectives  48.5 us (16%)
  waiting for transfers between devices  38.2 us (13%)
    psum x1, blocking collectives, per_device(): totals = lax.psum((cross_sum, self_sum), ('lat', 'prop'))  48.5 us
    ppermute x15, starting transfers between devices, per_device(): lax.ppermute(sent, 'prop', [(i_2, i_2 ^ step) for i_2 in range(length_2)])  48.3 us
    unnamed x50, local copies, waits for them, and re-layouts  27.1 us
    sub x28, other arithmetic, gain_step(): denom_imag = diag_now_imag - gain_imag  21.6 us
    sub x28, other arithmetic, gain_step(): denom_real = diag_now_real - gain_real  19.6 us
    ppermute x4, waiting for transfers between devices, extended(): after = lax.ppermute(first, axis, down)  14.8 us
    ppermute x15, waiting for transfers between devices, per_device(): lax.ppermute(sent, 'prop', [(i_2, i_2 ^ step) for i_2 in range(length_2)])  14.8 us
    ppermute x4, starting transfers between devices, extended(): before = lax.ppermute(last, axis, up)  12.3 us
  transfers between devices with their start and end apart: 25, of which 14 were waited for; matrix products, arithmetic and copies ran while one was open for 23% of the time, Pallas kernels for 0%

profile of v1, /device:TPU:0, one launch (start us, length us, event | category | flops | bytes accessed | tf_op | source)
XLA Modules:
  0.0 300.2 jit_solution(15742929061336354933)
XLA Ops:
  1.2 2.4 collective-permute-start
  7.6 7.7 %all-to-all-start = ((f32[16,1,128]{2,1,0:T(1,128)}), f32[16,1,128]{2,1,0:T(1,128)S(1)}, u32[]{:S(2)}, u32[]{:S(2)}) async-start(f32[16,1,128]{2,1,0:T(1,128)} %reshape.4051), calls=%async_computation | async-start | bytes 16384 | tf_op jit(solution)/shard_map/all_to_all | solution.py:167
  15.9 6.6 %all-to-all-done = f32[16,1,128]{2,1,0:T(1,128)S(1)} async-done(((f32[16,1,128]{2,1,0:T(1,128)}), f32[16,1,128]{2,1,0:T(1,128)S(1)}, u32[]{:S(2)}, u32[]{:S(2)}) %all-to-all-start) | async-done | bytes 8224 | tf_op jit(solution)/shard_map/all_to_all | solution.py:167
  25.0 2.5 collective-permute-start.2
  31.5 6.1 %collective-permute-done.3 = f32[2,3,16,1,4,128]{5,2,4,3,1,0:T(8,128)S(1)} collective-permute-done((f32[2,3,16,1,4,128]{5,2,4,3,1,0:T(8,128)S(1)}, f32[2,3,16,1,4,128]{5,2,4,3,1,0:T(8,128)S(1)}, u32[]{:S(2)}, u32[]{:S(2)}) %collective-permute-start.3) | collective-permute-done | bytes 196640 | tf_op jit(solution)/shard_map/ppermute | solution.py:31
  40.2 2.2 copy.274
  42.4 4.9 %reshape.4053 = f32[16,1,6144]{2,1,0:T(1,128)} reshape(f32[128,2,3,4,2,16]{5,4,3,2,1,0:T(2,128)S(1)} %bitcast.1690) | data formatting | bytes 786432
  47.3 3.8 %all-to-all-start.1 = ((f32[16,1,6144]{2,1,0:T(1,128)}), f32[16,1,6144]{2,1,0:T(1,128)S(1)}, u32[]{:S(2)}, u32[]{:S(2)}) async-start(f32[16,1,6144]{2,1,0:T(1,128)} %reshape.4053), calls=%async_computation.1 | async-start | bytes 786432 | tf_op jit(solution)/shard_map/all_to_all | solution.py:169
  51.2 44.6 %while.47 = (s32[]{:T(128)}, f32[16]{0:T(128)S(1)}, f32[16]{0:T(128)S(1)}, f32[4,16,16]{2,1,0:T(8,128)S(1)}, f32[4,16,16]{2,1,0:T(8,128)S(1)}, /*index=5*/f32[4,...) while((s32[]{:T(128)}, f32[16]{0:T(128)S(1)}, ...), condition=%wide.region_4.5_spmd.clone, body=%wide.region_3.4_spmd.clone.sunk | while | flops 2482 | bytes 45483 | solution.py:111
  97.4 2.4 reduce.1
  99.8 5.3 %reshape.4054 = f32[128,2,3,4,2,16]{5,4,3,2,1,0:T(2,128)S(1)} reshape(f32[16,6144]{1,0:T(8,128)} %reduce.1) | data formatting | bytes 786432
  106.4 2.3 copy.277
  108.7 2.5 reshape_reshape.6
  111.2 2.1 copy.278
  113.4 9.7 %while.45 = (s32[]{:T(128)}, f32[2,768]{1,0:T(2,128)S(1)}, f32[4,16,2,768]{3,2,1,0:T(2,128)S(1)}, f32[4,16,768]{2,1,0:T(8,128)S(1)}, f32[4,16,2,768]{3,2,1,0:T(2...) while((s32[]{:T(128)}, f32[2,768]{1,0:T(2,128)S(1)}, ...), condition=%wide.region_6.7_spmd, body=%wide.region_5.6_spmd.sunk | while | flops 124432 | bytes 719313 | solution.py:129
  123.3 2.9 while.46
  127.0 2.8 copy.279
  129.8 2.2 reshape_reshape.7
  132.0 2.5 copy.280
  134.9 2.0 collective-permute-start.4
  137.6 1.5 collective-permute-start.5
  139.2 1.9 collective-permute-start.7
  141.1 1.5 collective-permute-start.8
  142.5 2.7 collective-permute-start.9
  145.9 1.4 collective-permute-done.5
  149.0 2.4 collective-permute-start.11
  152.1 4.2 %collective-permute-start.12 = (f32[2,3,16,4,2,8]{2,5,4,3,1,0:T(8,128)S(1)}, f32[2,3,16,4,2,8]{2,5,4,3,1,0:T(8,128)S(1)}, u32[]{:S(2)}, u32[]{:S(2)}) collective-permute-start(f32[2,3,16,4,2,8]{2,5,4,3,1,0:T(8,128)S(1)} %get-tuple-element.453), channel_id=1, source_target_pairs={{0,9},{1,8},{2,11},{3,10},{4,13},{5,12},{6,15},{7,14},{8,1},{9,0},... | collective-permute-start | bytes 73736 | tf_op jit(solution)/shard_map/ppermute | solution.py:178
  157.0 2.0 collective-permute-done.8
  158.9 2.0 collective-permute-start.13
  161.7 3.2 %collective-permute-done.9 = f32[2,3,16,4,2,8]{2,5,4,3,1,0:T(8,128)S(1)} collective-permute-done((f32[2,3,16,4,2,8]{2,5,4,3,1,0:T(8,128)S(1)}, f32[2,3,16,4,2,8]{2,5,4,3,1,0:T(8,128)S(1)}, u32[]{:S(2)}, u32[]{:S(2)}) %collective-permute-start.9) | collective-permute-done | bytes 24608 | tf_op jit(solution)/shard_map/ppermute | solution.py:178
  164.8 1.9 collective-permute-start.14
  168.8 2.0 collective-permute-start.15
  171.4 17.5 %collective-permute-start.16 = (f32[2,3,16,4,2,8]{2,5,4,3,1,0:T(8,128)S(1)}, f32[2,3,16,4,2,8]{2,5,4,3,1,0:T(8,128)S(1)}, u32[]{:S(2)}, u32[]{:S(2)}) collective-permute-start(f32[2,3,16,4,2,8]{2,5,4,3,1,0:T(8,128)S(1)} %get-tuple-element.449), channel_id=1, source_target_pairs={{0,13},{1,12},{2,15},{3,14},{4,9},{5,8},{6,11},{7,10},{8,5},{9,4},... | collective-permute-start | bytes 73736 | tf_op jit(solution)/shard_map/ppermute | solution.py:178
  189.6 5.4 %collective-permute-done.12 = f32[2,3,16,4,2,8]{2,5,4,3,1,0:T(8,128)S(1)} collective-permute-done((f32[2,3,16,4,2,8]{2,5,4,3,1,0:T(8,128)S(1)}, f32[2,3,16,4,2,8]{2,5,4,3,1,0:T(8,128)S(1)}, u32[]{:S(2)}, u32[]{:S(2)}) %collective-permute-start.12) | collective-permute-done | bytes 24608 | tf_op jit(solution)/shard_map/ppermute | solution.py:178
  196.7 8.0 %collective-permute-start.18 = (f32[2,3,16,4,2,8]{2,5,4,3,1,0:T(8,128)S(1)}, f32[2,3,16,4,2,8]{2,5,4,3,1,0:T(8,128)S(1)}, u32[]{:S(2)}, u32[]{:S(2)}) collective-permute-start(f32[2,3,16,4,2,8]{2,5,4,3,1,0:T(8,128)S(1)} %get-tuple-element.447), channel_id=1, source_target_pairs={{0,15},{1,14},{2,13},{3,12},{4,11},{5,10},{6,9},{7,8},{8,7},{9,6},... | collective-permute-start | bytes 73736 | tf_op jit(solution)/shard_map/ppermute | solution.py:178
  209.1 2.8 gather_fusion
  212.3 1.6 copy-done
  213.9 1.9 fusion.386
  215.8 2.3 copy.284
  218.1 2.5 copy.282
  220.6 2.0 collective-permute-start.19
  222.6 2.5 copy.283
  226.8 1.9 collective-permute-done.20
  228.7 1.7 pad_maximum_fusion.7
  230.4 5.4 %collective-permute-start.21 = (f32[2,3,16,1,4,128]{5,2,4,3,1,0:T(8,128)}, f32[2,3,16,1,4,128]{5,2,4,3,1,0:T(8,128)}, u32[]{:S(2)}, u32[]{:S(2)}) collective-permute-start(f32[2,3,16,1,4,128]{5,2,4,3,1,0:T(8,128)} %get-tuple-element.475), channel_id=1, source_target_pairs={{0,1},{1,2},{2,3},{3,4},{4,5},{5,6},{6,7},{7,8},{8,9},{9,10},{10,1... | collective-permute-start | bytes 589832 | tf_op jit(solution)/shard_map/ppermute | solution.py:30
  239.8 6.8 %collective-permute-done.22 = f32[2,3,16,1,4,128]{5,2,4,3,1,0:T(8,128)} collective-permute-done((f32[2,3,16,1,4,128]{5,2,4,3,1,0:T(8,128)}, f32[2,3,16,1,4,128]{5,2,4,3,1,0:T(8,128)}, u32[]{:S(2)}, u32[]{:S(2)}) %collective-permute-start.22) | collective-permute-done | bytes 196640 | tf_op jit(solution)/shard_map/ppermute | solution.py:31
  246.7 1.9 select_maximum_fusion
  250.6 48.5 %all-reduce.2 = (f32[16]{0:T(128)S(1)}, f32[16]{0:T(128)S(1)}) all-reduce(f32[16]{0:T(128)S(1)} %get-tuple-element.268, f32[16]{0:T(128)S(1)} %get-tuple-element.267), channel_id=1, replica_groups=mesh['lat'=2,'prop'=16] {'lat','prop'}, use_global_device_ids=true, to_apply=%region_10.11 | all-reduce | flops 32 | bytes 256 | tf_op jit(solution)/shard_map/psum | solution.py:184
  (354 shorter events, 99.4 us)
Async XLA Ops:
  0.0 24.8 %copy-start.1 = (f32[2,3,16,4,2,128]{5,4,3,2,1,0:T(2,128)S(1)}, f32[2,3,16,4,2,128]{5,4,3,2,1,0:T(2,128)}, u32[]{:S(2)}) copy-start(f32[2,3,16,4,2,128]{5,4,3,2,1,0:T(2,128)} %param.15) | copy-start | bytes 1179652
  1.2 23.6 %collective-permute-start = (f32[2,3,16,4,1,128]{5,2,4,3,1,0:T(8,128)S(1)}, f32[2,3,16,4,1,128]{5,2,4,3,1,0:T(8,128)S(1)}, u32[]{:S(2)}, u32[]{:S(2)}) collective-permute-start(f32[2,3,16,4,1,128]{5,2,4,3,1,0:T(8,128)S(1)} %get-tuple-element.489), channel_id=1, source_target_pairs={{0,16},{1,17},{2,18},{3,19},{4,20},{5,21},{6,22},{7,23},{8,24},{9,... | collective-permute-start | bytes 589832 | tf_op jit(solution)/shard_map/ppermute | solution.py:30
  3.6 21.3 %collective-permute-start.1 = (f32[2,3,16,4,1,128]{5,2,4,3,1,0:T(8,128)S(1)}, f32[2,3,16,4,1,128]{5,2,4,3,1,0:T(8,128)S(1)}, u32[]{:S(2)}, u32[]{:S(2)}) collective-permute-start(f32[2,3,16,4,1,128]{5,2,4,3,1,0:T(8,128)S(1)} %get-tuple-element.488), channel_id=1, source_target_pairs={{16,0},{17,1},{18,2},{19,3},{20,4},{21,5},{22,6},{23,7},{24,8},{25... | collective-permute-start | bytes 589832 | tf_op jit(solution)/shard_map/ppermute | solution.py:31
  7.6 14.9 %all-to-all-start = ((f32[16,1,128]{2,1,0:T(1,128)}), f32[16,1,128]{2,1,0:T(1,128)S(1)}, u32[]{:S(2)}, u32[]{:S(2)}) async-start(f32[16,1,128]{2,1,0:T(1,128)} %reshape.4051), calls=%async_computation | async-start | bytes 16384 | tf_op jit(solution)/shard_map/all_to_all | solution.py:167
  25.0 6.5 %collective-permute-start.2 = (f32[2,3,16,1,4,128]{5,2,4,3,1,0:T(8,128)S(1)}, f32[2,3,16,1,4,128]{5,2,4,3,1,0:T(8,128)S(1)}, u32[]{:S(2)}, u32[]{:S(2)}) collective-permute-start(f32[2,3,16,1,4,128]{5,2,4,3,1,0:T(8,128)S(1)} %get-tuple-element.480), channel_id=1, source_target_pairs={{0,1},{1,2},{2,3},{3,4},{4,5},{5,6},{6,7},{7,8},{8,9},{9,10},{10,1... | collective-permute-start | bytes 589832 | tf_op jit(solution)/shard_map/ppermute | solution.py:30
  27.5 10.1 %collective-permute-start.3 = (f32[2,3,16,1,4,128]{5,2,4,3,1,0:T(8,128)S(1)}, f32[2,3,16,1,4,128]{5,2,4,3,1,0:T(8,128)S(1)}, u32[]{:S(2)}, u32[]{:S(2)}) collective-permute-start(f32[2,3,16,1,4,128]{5,2,4,3,1,0:T(8,128)S(1)} %get-tuple-element.481), channel_id=1, source_target_pairs={{1,0},{2,1},{3,2},{4,3},{5,4},{6,5},{7,6},{8,7},{9,8},{10,9},{11,1... | collective-permute-start | bytes 589832 | tf_op jit(solution)/shard_map/ppermute | solution.py:31
  38.9 1.2 copy-start.8
  39.3 0.7 copy-start.3
  39.3 0.8 copy-start.5
  42.4 8.7 %copy-start.12 = (f32[4,16,16]{2,1,0:T(8,128)S(1)}, f32[4,16,16]{2,1,0:T(8,128)}, u32[]{:S(2)}) copy-start(f32[4,16,16]{2,1,0:T(8,128)} %custom-call.8) | copy-start | bytes 12292
  42.4 8.7 %copy-start.13 = (f32[4,16,16]{2,1,0:T(8,128)S(1)}, f32[4,16,16]{2,1,0:T(8,128)}, u32[]{:S(2)}) copy-start(f32[4,16,16]{2,1,0:T(8,128)} %custom-call.9) | copy-start | bytes 12292
  47.3 50.0 %all-to-all-start.1 = ((f32[16,1,6144]{2,1,0:T(1,128)}), f32[16,1,6144]{2,1,0:T(1,128)S(1)}, u32[]{:S(2)}, u32[]{:S(2)}) async-start(f32[16,1,6144]{2,1,0:T(1,128)} %reshape.4053), calls=%async_computation.1 | async-start | bytes 786432 | tf_op jit(solution)/shard_map/all_to_all | solution.py:169
  126.2 0.7 copy-start.7
  134.9 7.6 %collective-permute-start.4 = (f32[2,3,16,4,2,8]{2,5,4,3,1,0:T(8,128)S(1)}, f32[2,3,16,4,2,8]{2,5,4,3,1,0:T(8,128)S(1)}, u32[]{:S(2)}, u32[]{:S(2)}) collective-permute-start(f32[2,3,16,4,2,8]{2,5,4,3,1,0:T(8,128)S(1)} %get-tuple-element.461), channel_id=1, source_target_pairs={{0,1},{1,0},{2,3},{3,2},{4,5},{5,4},{6,7},{7,6},{8,9},{9,8},{10,11... | collective-permute-start | bytes 73736 | tf_op jit(solution)/shard_map/ppermute | solution.py:178
  137.6 9.7 %collective-permute-start.5 = (f32[2,3,16,4,2,8]{2,5,4,3,1,0:T(8,128)S(1)}, f32[2,3,16,4,2,8]{2,5,4,3,1,0:T(8,128)S(1)}, u32[]{:S(2)}, u32[]{:S(2)}) collective-permute-start(f32[2,3,16,4,2,8]{2,5,4,3,1,0:T(8,128)S(1)} %get-tuple-element.460), channel_id=1, source_target_pairs={{0,2},{1,3},{2,0},{3,1},{4,6},{5,7},{6,4},{7,5},{8,10},{9,11},{10,... | collective-permute-start | bytes 73736 | tf_op jit(solution)/shard_map/ppermute | solution.py:178
  139.0 10.0 %collective-permute-start.6 = (f32[2,3,16,4,2,8]{2,5,4,3,1,0:T(8,128)S(1)}, f32[2,3,16,4,2,8]{2,5,4,3,1,0:T(8,128)S(1)}, u32[]{:S(2)}, u32[]{:S(2)}) collective-permute-start(f32[2,3,16,4,2,8]{2,5,4,3,1,0:T(8,128)S(1)} %get-tuple-element.459), channel_id=1, source_target_pairs={{0,3},{1,2},{2,1},{3,0},{4,7},{5,6},{6,5},{7,4},{8,11},{9,10},{10,... | collective-permute-start | bytes 73736 | tf_op jit(solution)/shard_map/ppermute | solution.py:178
  139.2 13.0 %collective-permute-start.7 = (f32[2,3,16,4,2,8]{2,5,4,3,1,0:T(8,128)S(1)}, f32[2,3,16,4,2,8]{2,5,4,3,1,0:T(8,128)S(1)}, u32[]{:S(2)}, u32[]{:S(2)}) collective-permute-start(f32[2,3,16,4,2,8]{2,5,4,3,1,0:T(8,128)S(1)} %get-tuple-element.458), channel_id=1, source_target_pairs={{0,4},{1,5},{2,6},{3,7},{4,0},{5,1},{6,2},{7,3},{8,12},{9,13},{10,... | collective-permute-start | bytes 73736 | tf_op jit(solution)/shard_map/ppermute | solution.py:178
  141.1 17.9 %collective-permute-start.8 = (f32[2,3,16,4,2,8]{2,5,4,3,1,0:T(8,128)S(1)}, f32[2,3,16,4,2,8]{2,5,4,3,1,0:T(8,128)S(1)}, u32[]{:S(2)}, u32[]{:S(2)}) collective-permute-start(f32[2,3,16,4,2,8]{2,5,4,3,1,0:T(8,128)S(1)} %get-tuple-element.457), channel_id=1, source_target_pairs={{0,5},{1,4},{2,7},{3,6},{4,1},{5,0},{6,3},{7,2},{8,13},{9,12},{10,... | collective-permute-start | bytes 73736 | tf_op jit(solution)/shard_map/ppermute | solution.py:178
  142.5 22.3 %collective-permute-start.9 = (f32[2,3,16,4,2,8]{2,5,4,3,1,0:T(8,128)S(1)}, f32[2,3,16,4,2,8]{2,5,4,3,1,0:T(8,128)S(1)}, u32[]{:S(2)}, u32[]{:S(2)}) collective-permute-start(f32[2,3,16,4,2,8]{2,5,4,3,1,0:T(8,128)S(1)} %get-tuple-element.456), channel_id=1, source_target_pairs={{0,6},{1,7},{2,4},{3,5},{4,2},{5,3},{6,0},{7,1},{8,14},{9,15},{10,... | collective-permute-start | bytes 73736 | tf_op jit(solution)/shard_map/ppermute | solution.py:178
  147.3 21.5 %collective-permute-start.10 = (f32[2,3,16,4,2,8]{2,5,4,3,1,0:T(8,128)S(1)}, f32[2,3,16,4,2,8]{2,5,4,3,1,0:T(8,128)S(1)}, u32[]{:S(2)}, u32[]{:S(2)}) collective-permute-start(f32[2,3,16,4,2,8]{2,5,4,3,1,0:T(8,128)S(1)} %get-tuple-element.455), channel_id=1, source_target_pairs={{0,7},{1,6},{2,5},{3,4},{4,3},{5,2},{6,1},{7,0},{8,15},{9,14},{10,... | collective-permute-start | bytes 73736 | tf_op jit(solution)/shard_map/ppermute | solution.py:178
  149.0 22.4 %collective-permute-start.11 = (f32[2,3,16,4,2,8]{2,5,4,3,1,0:T(8,128)S(1)}, f32[2,3,16,4,2,8]{2,5,4,3,1,0:T(8,128)S(1)}, u32[]{:S(2)}, u32[]{:S(2)}) collective-permute-start(f32[2,3,16,4,2,8]{2,5,4,3,1,0:T(8,128)S(1)} %get-tuple-element.454), channel_id=1, source_target_pairs={{0,8},{1,9},{2,10},{3,11},{4,12},{5,13},{6,14},{7,15},{8,0},{9,1},... | collective-permute-start | bytes 73736 | tf_op jit(solution)/shard_map/ppermute | solution.py:178
  152.1 42.9 %collective-permute-start.12 = (f32[2,3,16,4,2,8]{2,5,4,3,1,0:T(8,128)S(1)}, f32[2,3,16,4,2,8]{2,5,4,3,1,0:T(8,128)S(1)}, u32[]{:S(2)}, u32[]{:S(2)}) collective-permute-start(f32[2,3,16,4,2,8]{2,5,4,3,1,0:T(8,128)S(1)} %get-tuple-element.453), channel_id=1, source_target_pairs={{0,9},{1,8},{2,11},{3,10},{4,13},{5,12},{6,15},{7,14},{8,1},{9,0},... | collective-permute-start | bytes 73736 | tf_op jit(solution)/shard_map/ppermute | solution.py:178
  158.9 37.8 %collective-permute-start.13 = (f32[2,3,16,4,2,8]{2,5,4,3,1,0:T(8,128)S(1)}, f32[2,3,16,4,2,8]{2,5,4,3,1,0:T(8,128)S(1)}, u32[]{:S(2)}, u32[]{:S(2)}) collective-permute-start(f32[2,3,16,4,2,8]{2,5,4,3,1,0:T(8,128)S(1)} %get-tuple-element.452), channel_id=1, source_target_pairs={{0,10},{1,11},{2,8},{3,9},{4,14},{5,15},{6,12},{7,13},{8,2},{9,3},... | collective-permute-start | bytes 73736 | tf_op jit(solution)/shard_map/ppermute | solution.py:178
  164.8 40.6 %collective-permute-start.14 = (f32[2,3,16,4,2,8]{2,5,4,3,1,0:T(8,128)S(1)}, f32[2,3,16,4,2,8]{2,5,4,3,1,0:T(8,128)S(1)}, u32[]{:S(2)}, u32[]{:S(2)}) collective-permute-start(f32[2,3,16,4,2,8]{2,5,4,3,1,0:T(8,128)S(1)} %get-tuple-element.451), channel_id=1, source_target_pairs={{0,11},{1,10},{2,9},{3,8},{4,15},{5,14},{6,13},{7,12},{8,3},{9,2},... | collective-permute-start | bytes 73736 | tf_op jit(solution)/shard_map/ppermute | solution.py:178
  168.8 37.3 %collective-permute-start.15 = (f32[2,3,16,4,2,8]{2,5,4,3,1,0:T(8,128)S(1)}, f32[2,3,16,4,2,8]{2,5,4,3,1,0:T(8,128)S(1)}, u32[]{:S(2)}, u32[]{:S(2)}) collective-permute-start(f32[2,3,16,4,2,8]{2,5,4,3,1,0:T(8,128)S(1)} %get-tuple-element.450), channel_id=1, source_target_pairs={{0,12},{1,13},{2,14},{3,15},{4,8},{5,9},{6,10},{7,11},{8,4},{9,5},... | collective-permute-start | bytes 73736 | tf_op jit(solution)/shard_map/ppermute | solution.py:178
  171.4 35.4 %collective-permute-start.16 = (f32[2,3,16,4,2,8]{2,5,4,3,1,0:T(8,128)S(1)}, f32[2,3,16,4,2,8]{2,5,4,3,1,0:T(8,128)S(1)}, u32[]{:S(2)}, u32[]{:S(2)}) collective-permute-start(f32[2,3,16,4,2,8]{2,5,4,3,1,0:T(8,128)S(1)} %get-tuple-element.449), channel_id=1, source_target_pairs={{0,13},{1,12},{2,15},{3,14},{4,9},{5,8},{6,11},{7,10},{8,5},{9,4},... | collective-permute-start | bytes 73736 | tf_op jit(solution)/shard_map/ppermute | solution.py:178
  195.0 12.5 %collective-permute-start.17 = (f32[2,3,16,4,2,8]{2,5,4,3,1,0:T(8,128)S(1)}, f32[2,3,16,4,2,8]{2,5,4,3,1,0:T(8,128)S(1)}, u32[]{:S(2)}, u32[]{:S(2)}) collective-permute-start(f32[2,3,16,4,2,8]{2,5,4,3,1,0:T(8,128)S(1)} %get-tuple-element.448), channel_id=1, source_target_pairs={{0,14},{1,15},{2,12},{3,13},{4,10},{5,11},{6,8},{7,9},{8,6},{9,7},... | collective-permute-start | bytes 73736 | tf_op jit(solution)/shard_map/ppermute | solution.py:178
  196.7 11.7 %collective-permute-start.18 = (f32[2,3,16,4,2,8]{2,5,4,3,1,0:T(8,128)S(1)}, f32[2,3,16,4,2,8]{2,5,4,3,1,0:T(8,128)S(1)}, u32[]{:S(2)}, u32[]{:S(2)}) collective-permute-start(f32[2,3,16,4,2,8]{2,5,4,3,1,0:T(8,128)S(1)} %get-tuple-element.447), channel_id=1, source_target_pairs={{0,15},{1,14},{2,13},{3,12},{4,11},{5,10},{6,9},{7,8},{8,7},{9,6},... | collective-permute-start | bytes 73736 | tf_op jit(solution)/shard_map/ppermute | solution.py:178
  212.3 1.6 copy-start
  220.6 6.2 %collective-permute-start.19 = (f32[2,3,16,4,1,128]{5,2,4,3,1,0:T(8,128)}, f32[2,3,16,4,1,128]{5,2,4,3,1,0:T(8,128)}, u32[]{:S(2)}, u32[]{:S(2)}) collective-permute-start(f32[2,3,16,4,1,128]{5,2,4,3,1,0:T(8,128)} %copy.282), channel_id=1, source_target_pairs={{0,16},{1,17},{2,18},{3,19},{4,20},{5,21},{6,22},{7,23},{8,24},{9,... | collective-permute-start | bytes 589832 | tf_op jit(solution)/shard_map/ppermute | solution.py:30
  225.1 3.5 %collective-permute-start.20 = (f32[2,3,16,4,1,128]{5,2,4,3,1,0:T(8,128)}, f32[2,3,16,4,1,128]{5,2,4,3,1,0:T(8,128)S(1)}, u32[]{:S(2)}, u32[]{:S(2)}) collective-permute-start(f32[2,3,16,4,1,128]{5,2,4,3,1,0:T(8,128)} %copy.283), channel_id=1, source_target_pairs={{16,0},{17,1},{18,2},{19,3},{20,4},{21,5},{22,6},{23,7},{24,8},{25... | collective-permute-start | bytes 589832 | tf_op jit(solution)/shard_map/ppermute | solution.py:31
  228.7 8.8 %copy-start.11 = (f32[2,3,16,4,1,128]{5,2,4,3,1,0:T(8,128)}, f32[2,3,16,4,1,128]{5,2,4,3,1,0:T(8,128)S(1)}, u32[]{:S(2)}) copy-start(f32[2,3,16,4,1,128]{5,2,4,3,1,0:T(8,128)S(1)} %collective-permute-done.20) | copy-start | bytes 589828
  230.4 9.5 %collective-permute-start.21 = (f32[2,3,16,1,4,128]{5,2,4,3,1,0:T(8,128)}, f32[2,3,16,1,4,128]{5,2,4,3,1,0:T(8,128)}, u32[]{:S(2)}, u32[]{:S(2)}) collective-permute-start(f32[2,3,16,1,4,128]{5,2,4,3,1,0:T(8,128)} %get-tuple-element.475), channel_id=1, source_target_pairs={{0,1},{1,2},{2,3},{3,4},{4,5},{5,6},{6,7},{7,8},{8,9},{9,10},{10,1... | collective-permute-start | bytes 589832 | tf_op jit(solution)/shard_map/ppermute | solution.py:30
  235.7 10.9 %collective-permute-start.22 = (f32[2,3,16,1,4,128]{5,2,4,3,1,0:T(8,128)}, f32[2,3,16,1,4,128]{5,2,4,3,1,0:T(8,128)}, u32[]{:S(2)}, u32[]{:S(2)}) collective-permute-start(f32[2,3,16,1,4,128]{5,2,4,3,1,0:T(8,128)} %get-tuple-element.476), channel_id=1, source_target_pairs={{1,0},{2,1},{3,2},{4,3},{5,4},{6,5},{7,6},{8,7},{9,8},{10,9},{11,1... | collective-permute-start | bytes 589832 | tf_op jit(solution)/shard_map/ppermute | solution.py:31
  248.8 0.9 copy-start.10
  249.2 1.0 copy-start.4
  249.2 1.0 copy-start.6
  249.2 1.2 copy-start.9
  249.2 50.0 %copy-start.2 = (f32[2,3,16,4,2,128]{5,4,3,2,1,0:T(2,128)S(1)}, f32[2,3,16,4,2,128]{5,4,3,2,1,0:T(2,128)}, u32[]{:S(2)}) copy-start(f32[2,3,16,4,2,128]{5,4,3,2,1,0:T(2,128)} %param.15) | copy-start | bytes 1179652
